TPU v7x, 32 devices: a whole 2x2x4 slice. The times are simulated.
32 devices in a mesh: seq: 16 (over z, y, x), dp: 2 (over core).
Axes of the slice: x: 2, y: 2, z: 4, core: 2. Of those that a mesh axis runs over, the one named last changes fastest.
Arguments:
- inputs: bfloat16 [8, 1536, 896], P('dp', 'seq'), may hold values from -6 to 6
- lengths: int32 [8, 9], P('dp'), may hold values from 0 to 1536, as said below
- w_qkv: bfloat16 [896, 1152], replicated, may hold values from -0.1875 to 0.1875
- b_qkv: bfloat16 [1152], replicated, may hold values from -3 to 3
- g_attn: bfloat16 [896], replicated, may hold values from 0.25 to 1.75
- w_out: bfloat16 [896, 896], replicated, may hold values from -1.5 to 1.5
- g_mlp: bfloat16 [896], replicated, may hold values from 0.25 to 1.75
- w_gate_up: bfloat16 [896, 9728], replicated, may hold values from -0.1875 to 0.1875
- w_down: bfloat16 [4864, 896], replicated, may hold values from -0.078125 to 0.078125
- cotangent: bfloat16 [8, 1536, 896], P('dp', 'seq'), may hold values from -6 to 6
Outputs:
- output: bfloat16 [8, 1536, 896], P('dp', 'seq')
- grad_input: float32 [8, 1536, 896], P('dp', 'seq')
- grad_qkv: float32 [896, 1152], P('seq')
- grad_bias_qkv: float32 [1152], replicated
- grad_norm_attn: float32 [896], replicated
- grad_out: float32 [896, 896], P('seq')
- grad_norm_mlp: float32 [896], replicated
- grad_gate_up: float32 [896, 9728], P('seq')
- grad_down: float32 [4864, 896], P('seq')
Inputs may be any that keep to these rules, and one draw needn't show every extreme that they name: Each row lists the lengths of the documents packed one after another from the start of a stream; nonzero entries come first, and the tokens after their sum, fewer than 96, are padding. In every group of 4 consecutive rows one row is a single document of 1536 tokens; any other document has at most 4096 tokens.
All inputs are finite; a program needn't handle non-finite values.
Results may differ from a plain program's by a relative error of at most 0.014.
Values may be sent and summed in bfloat16 or wider, within the bound.
No kernel may reach another device: no remote copies, remote signals or barrier semaphores. Data moves between devices by JAX's collectives and lax.ppermute only.
A program may use at most 576 MiB of HBM per device.

v0:
```python
import jax
import jax.numpy as jnp
from jax import lax
from jax.sharding import PartitionSpec as P

HEADS = 14
KVH = 2
HD = 64
FF = 4864
epsilon = 1e-06
rope_base = 1000000.0


def cut_along(shard, dim, devices):
    before, after = (shard.shape[:dim], shard.shape[dim + 1 :])
    return jnp.moveaxis(shard.reshape(*before, devices, -1, *after), dim, 0)


def summed_on_arrival(shard, axis, dim):
    devices = lax.axis_size(axis)
    blocks = lax.all_to_all(cut_along(shard, dim, devices), axis, 0, 0, tiled=True)
    return jnp.sum(blocks.astype(jnp.float32), axis=0)


def layout(lengths, offset, row_count):
    places = offset + jnp.arange(row_count, dtype=jnp.int32)
    ends = jnp.cumsum(lengths, axis=-1, dtype=jnp.int32)
    after = (places[None, :, None] >= ends[:, None, :]).astype(jnp.int32)
    segment = jnp.sum(after, axis=-1, dtype=jnp.int32)
    begins = jnp.sum(after * lengths[:, None, :], axis=-1, dtype=jnp.int32)
    return (segment, places[None, :] - begins, places[None, :] < ends[:, -1:])


def tables(position, head_size):
    half = head_size // 2
    inverse = rope_base ** (-(jnp.arange(half, dtype=jnp.float32) * (2.0 / head_size)))
    angle = position.astype(jnp.float32)[..., None] * inverse
    return (jnp.cos(angle)[..., None, :], jnp.sin(angle)[..., None, :])


def rotate(field, cos_table, sin_table):
    half = field.shape[-1] // 2
    first = field[..., :half]
    second = field[..., half:]
    return jnp.concatenate(
        [first * cos_table - second * sin_table, second * cos_table + first * sin_table], axis=-1
    )


def unrotate(grad_field, cos_table, sin_table):
    half = grad_field.shape[-1] // 2
    first = grad_field[..., :half]
    second = grad_field[..., half:]
    return jnp.concatenate(
        [first * cos_table + second * sin_table, second * cos_table - first * sin_table], axis=-1
    )


def transposed_product(left, right):
    return lax.dot_general(
        left, right, (((1,), (1,)), ((), ())), preferred_element_type=jnp.float32
    )


def shards(inputs, lengths, w_qkv, b_qkv, g_attn, w_out, g_mlp, w_gate_up, w_down, cotangent):
    streams, length, model_width = inputs.shape
    tokens = streams * length
    stream_len = length * lax.axis_size("seq")
    offset = lax.axis_index("seq") * length
    q_width = HEADS * HD
    kv_width = KVH * HD
    group_size = HEADS // KVH
    factor = HD ** (-0.5)
    blocks = max(1, min(16, stream_len // 512))
    key_block = stream_len // blocks
    q_seg, q_pos, valid_rows = layout(lengths, offset, length)
    k_seg, unused_pos, unused_valid = layout(lengths, 0, stream_len)
    q_place = offset + jnp.arange(length, dtype=jnp.int32)
    residual = inputs.reshape(tokens, model_width).astype(jnp.float32)
    inv_attn = lax.rsqrt(jnp.mean(residual * residual, axis=-1, keepdims=True) + epsilon)
    unit_attn = residual * inv_attn
    gain_attn = g_attn.astype(jnp.float32)
    normed = (unit_attn * gain_attn).astype(jnp.bfloat16)
    projected = jnp.dot(normed, w_qkv, preferred_element_type=jnp.float32) + b_qkv.astype(
        jnp.float32
    )
    cos_table, sin_table = tables(q_pos.reshape(tokens), HD)
    q_rot = rotate(projected[:, :q_width].reshape(tokens, HEADS, HD), cos_table, sin_table)
    k_rot = rotate(
        projected[:, q_width : q_width + kv_width].reshape(tokens, KVH, HD), cos_table, sin_table
    )
    queries = q_rot.astype(jnp.bfloat16).reshape(streams, length, KVH, group_size, HD)
    key_low = k_rot.astype(jnp.bfloat16).reshape(streams, length, kv_width)
    value_low = (
        projected[:, q_width + kv_width :].astype(jnp.bfloat16).reshape(streams, length, kv_width)
    )
    key_all, value_all = (
        lax.all_gather(key_low, "seq", axis=1, tiled=True),
        lax.all_gather(value_low, "seq", axis=1, tiled=True),
    )
    key_all = key_all.reshape(streams, stream_len, KVH, HD)
    value_all = value_all.reshape(streams, stream_len, KVH, HD)

    def scored(key_part, key_seg, first_key, rows):
        scores = (
            jnp.einsum("bqhgd,bkhd->bhgqk", queries, key_part, preferred_element_type=jnp.float32)
            * factor
        )
        key_place = first_key + jnp.arange(rows, dtype=jnp.int32)
        allowed = (q_seg[:, :, None] == key_seg[:, None, :]) & (
            q_place[None, :, None] >= key_place[None, None, :]
        )
        return (scores, allowed[:, None, None])

    def touches(first_key, rows):
        last_seg = lax.dynamic_slice_in_dim(k_seg, first_key + rows - 1, 1, 1)[:, 0]
        return jnp.any((first_key <= q_place[length - 1]) & (last_seg >= q_seg[:, 0]))

    def slices(first_key, rows, key_src, value_src):
        return (
            lax.dynamic_slice_in_dim(key_src, first_key, rows, 1),
            lax.dynamic_slice_in_dim(value_src, first_key, rows, 1),
            lax.dynamic_slice_in_dim(k_seg, first_key, rows, 1),
        )

    def softmax_stats(block_index, running):
        first_key = block_index * key_block

        def softmax_compute(state):
            row_max, row_sum = state
            key_part, unused_value, key_seg = slices(first_key, key_block, key_all, value_all)
            scores, allowed = scored(key_part, key_seg, first_key, key_block)
            masked = jnp.where(allowed, scores, -1e30)
            new_max = jnp.maximum(row_max, jnp.max(masked, axis=-1, keepdims=True))
            fresh = jnp.where(allowed, jnp.exp(masked - new_max), 0.0)
            return (
                new_max,
                row_sum * jnp.exp(row_max - new_max) + jnp.sum(fresh, axis=-1, keepdims=True),
            )

        return lax.cond(
            touches(first_key, key_block), softmax_compute, lambda state: state, running
        )

    stat_shape = (streams, KVH, group_size, length, 1)
    row_max, row_sum = lax.fori_loop(
        0,
        blocks,
        softmax_stats,
        (jnp.full(stat_shape, -1e30, jnp.float32), jnp.zeros(stat_shape, jnp.float32)),
    )
    log_sum = row_max + jnp.log(row_sum)

    def weighted(block_index, running):
        first_key = block_index * key_block

        def weighted_compute(partial_value):
            key_part, value_part, key_seg = slices(first_key, key_block, key_all, value_all)
            scores, allowed = scored(key_part, key_seg, first_key, key_block)
            weights = jnp.where(allowed, jnp.exp(scores - log_sum), 0.0).astype(jnp.bfloat16)
            return partial_value + jnp.einsum(
                "bhgqk,bkhd->bqhgd", weights, value_part, preferred_element_type=jnp.float32
            )

        return lax.cond(
            touches(first_key, key_block),
            weighted_compute,
            lambda partial_value: partial_value,
            running,
        )

    mixed_out = lax.fori_loop(
        0, blocks, weighted, jnp.zeros((streams, length, KVH, group_size, HD), jnp.float32)
    )
    mixed_low = mixed_out.reshape(tokens, q_width).astype(jnp.bfloat16)
    middle = residual + jnp.dot(mixed_low, w_out, preferred_element_type=jnp.float32)
    inv_mlp = lax.rsqrt(jnp.mean(middle * middle, axis=-1, keepdims=True) + epsilon)
    unit_mlp = middle * inv_mlp
    gain_mlp = g_mlp.astype(jnp.float32)
    normed_mlp = (unit_mlp * gain_mlp).astype(jnp.bfloat16)
    gate_up = jnp.dot(normed_mlp, w_gate_up, preferred_element_type=jnp.float32)
    gate_pre = gate_up[:, :FF]
    up_pre = gate_up[:, FF:]
    gate_sigmoid = jax.nn.sigmoid(gate_pre)
    gate_silu = jax.nn.silu(gate_pre)
    active = (gate_silu * up_pre).astype(jnp.bfloat16)
    output = (middle + jnp.dot(active, w_down, preferred_element_type=jnp.float32)).astype(
        jnp.bfloat16
    )
    seed_grad = (cotangent * valid_rows[..., None].astype(jnp.bfloat16)).reshape(
        tokens, model_width
    )
    grad_active = transposed_product(seed_grad, w_down)
    grad_gate = grad_active * up_pre * (gate_sigmoid * (1.0 + gate_pre * (1.0 - gate_sigmoid)))
    grad_up = grad_active * gate_silu
    grad_gate_up = jnp.concatenate([grad_gate, grad_up], axis=1).astype(jnp.bfloat16)
    grad_normed_mlp = transposed_product(grad_gate_up, w_gate_up)
    scaled_mlp = grad_normed_mlp * gain_mlp
    grad_middle = seed_grad.astype(jnp.float32) + inv_mlp * (
        scaled_mlp - unit_mlp * jnp.mean(scaled_mlp * unit_mlp, axis=-1, keepdims=True)
    )
    gain_mlp_part = jnp.sum(grad_normed_mlp * unit_mlp, axis=0)
    grad_branch = grad_middle.astype(jnp.bfloat16)
    grad_mixed = (
        transposed_product(grad_branch, w_out)
        .astype(jnp.bfloat16)
        .reshape(streams, length, KVH, group_size, HD)
    )
    row_delta = jnp.sum(grad_mixed.astype(jnp.float32) * mixed_out, axis=-1).transpose(0, 2, 3, 1)[
        ..., None
    ]
    key_back, value_back = (
        lax.all_gather(key_low, "seq", axis=1, tiled=True),
        lax.all_gather(value_low, "seq", axis=1, tiled=True),
    )
    key_back = key_back.reshape(streams, stream_len, KVH, HD)
    value_back = value_back.reshape(streams, stream_len, KVH, HD)

    def back_block(block_index, running):
        first_key = block_index * key_block

        def back_compute(state):
            query_grads, key_terms_all = state
            key_part, value_part, key_seg = slices(first_key, key_block, key_back, value_back)
            scores, allowed = scored(key_part, key_seg, first_key, key_block)
            weights = jnp.where(allowed, jnp.exp(scores - log_sum), 0.0)
            grad_weights = jnp.einsum(
                "bqhgd,bkhd->bhgqk", grad_mixed, value_part, preferred_element_type=jnp.float32
            )
            grad_scores = (weights * (grad_weights - row_delta)).astype(jnp.bfloat16)
            query_grads = (
                query_grads
                + jnp.einsum(
                    "bhgqk,bkhd->bqhgd", grad_scores, key_part, preferred_element_type=jnp.float32
                )
                * factor
            )
            grad_keys = (
                jnp.einsum(
                    "bhgqk,bqhgd->kbhd", grad_scores, queries, preferred_element_type=jnp.float32
                )
                * factor
            )
            grad_values = jnp.einsum(
                "bhgqk,bqhgd->kbhd",
                weights.astype(jnp.bfloat16),
                grad_mixed,
                preferred_element_type=jnp.float32,
            )
            piece = jnp.concatenate(
                [
                    grad_keys.reshape(key_block, streams, kv_width),
                    grad_values.reshape(key_block, streams, kv_width),
                ],
                axis=-1,
            )
            key_terms_all = lax.dynamic_update_slice_in_dim(key_terms_all, piece, first_key, 0)
            return (query_grads, key_terms_all)

        return lax.cond(touches(first_key, key_block), back_compute, lambda state: state, running)

    grad_queries, key_terms_all = lax.fori_loop(
        0,
        blocks,
        back_block,
        (
            jnp.zeros((streams, length, KVH, group_size, HD), jnp.float32),
            jnp.zeros((stream_len, streams, 2 * kv_width), jnp.float32),
        ),
    )
    key_grads = summed_on_arrival(key_terms_all.astype(jnp.bfloat16), "seq", 0)
    key_grads = key_grads.transpose(1, 0, 2).reshape(tokens, 2 * kv_width)
    grad_q_lin = unrotate(grad_queries.reshape(tokens, HEADS, HD), cos_table, sin_table).reshape(
        tokens, q_width
    )
    grad_k_lin = unrotate(
        key_grads[:, :kv_width].reshape(tokens, KVH, HD), cos_table, sin_table
    ).reshape(tokens, kv_width)
    grad_projected = jnp.concatenate(
        [grad_q_lin, grad_k_lin, key_grads[:, kv_width:]], axis=1
    ).astype(jnp.bfloat16)
    grad_normed = transposed_product(grad_projected, w_qkv)
    scaled_attn = grad_normed * gain_attn
    grad_input = grad_middle + inv_attn * (
        scaled_attn - unit_attn * jnp.mean(scaled_attn * unit_attn, axis=-1, keepdims=True)
    )
    gain_attn_part = jnp.sum(grad_normed * unit_attn, axis=0)
    bias_part = jnp.sum(grad_projected.astype(jnp.float32), axis=0)

    def make_rows():

        def product(left, right):
            return lax.dot_general(
                left, right, (((0,), (0,)), ((), ())), preferred_element_type=jnp.float32
            )

        def row_terms(first_col, col_count):
            return jnp.concatenate(
                [
                    product(normed, grad_projected),
                    product(mixed_low, grad_branch),
                    product(normed_mlp, grad_gate_up),
                ],
                axis=1,
            )

        def down_terms(first_col, col_count):
            return product(active, seed_grad)

        return (row_terms, down_terms)

    row_share = model_width // lax.axis_size("seq")
    hidden_share = FF // lax.axis_size("seq")
    row_terms, down_terms = make_rows()
    row_part = lax.psum_scatter(
        row_terms(jnp.int32(0), row_share * lax.axis_size("seq")),
        "seq",
        scatter_dimension=0,
        tiled=True,
    )
    down_part = summed_on_arrival(
        down_terms(jnp.int32(0), hidden_share * lax.axis_size("seq")).astype(jnp.bfloat16), "seq", 0
    )
    row_part, down_part = (
        lax.psum(row_part.astype(jnp.bfloat16), "dp").astype(jnp.float32),
        lax.psum(down_part.astype(jnp.bfloat16), "dp").astype(jnp.float32),
    )
    bias_grad, gain_attn_grad, gain_mlp_grad = lax.psum(
        (bias_part, gain_attn_part, gain_mlp_part), ("seq", "dp")
    )
    joined_width = q_width + 2 * kv_width
    return (
        output.reshape(streams, length, model_width),
        grad_input.reshape(streams, length, model_width),
        row_part[:, :joined_width],
        bias_grad,
        gain_attn_grad,
        row_part[:, joined_width : joined_width + model_width],
        gain_mlp_grad,
        row_part[:, joined_width + model_width :],
        down_part,
    )


def solution(mesh):
    in_specs = (
        P("dp", "seq", None),
        P("dp", None),
        P(),
        P(),
        P(),
        P(),
        P(),
        P(),
        P(),
        P("dp", "seq", None),
    )
    out_specs = (
        P("dp", "seq", None),
        P("dp", "seq", None),
        P("seq", None),
        P(),
        P(),
        P("seq", None),
        P(),
        P("seq", None),
        P("seq", None),
    )
    return jax.shard_map(shards, mesh=mesh, in_specs=in_specs, out_specs=out_specs, check_vma=False)
```

profile of v0, /device:TPU:6, one launch (start us, length us, event | category | flops | bytes accessed | tf_op | source)
XLA Modules:
  0.0 1464.1 jit_solution(16891637317464104812)
XLA Ops:
  29.2 46.4 %all-gather.5.cloned.1.call-done = bf16[4,1536,128]{2,0,1:T(4,128)(2,1)} async-done(((bf16[4,96,128]{2,0,1:T(4,128)(2,1)}), bf16[4,1536,128]{2,0,1:T(4,128)(2,1)}) %all-gather.5.cloned.1.call-update) | async-done | bytes 1572880 | tf_op jit(solution)/shard_map/all_gather | solution.py:98
  79.5 15.1 %while.58 = (s32[]{:T(128)}, f32[4,2,7,96,1]{3,2,1,0,4:T(8,128)S(1)}, f32[4,2,7,96,1]{3,2,1,0,4:T(8,128)S(1)}, s32[96]{0:T(128)S(1)}, s32[4,1536]{1,0:T(4,128)S(...) while((s32[]{:T(128)}, ...), condition=%wide.region_11.12_spmd, body=%wide.region_5.11_spmd.sunk | while | flops 374795296 | bytes 24231176 | solution.py:146
  82.1 7.2 conditional.6
  94.6 40.9 %all-gather.3.cloned.1.call-done = bf16[4,1536,128]{2,1,0:T(8,128)(2,1)} async-done(((bf16[4,96,128]{2,1,0:T(8,128)(2,1)}), bf16[4,1536,128]{2,1,0:T(8,128)(2,1)}) %all-gather.3.cloned.1.call-update) | async-done | bytes 1572880 | tf_op jit(solution)/shard_map/all_gather | solution.py:99
  139.5 15.9 %while.59 = (s32[]{:T(128)}, f32[4,96,2,7,64]{1,4,3,2,0:T(8,128)}, s32[96]{0:T(128)S(1)}, s32[4,1536]{1,0:T(4,128)S(1)}, s32[4,96]{1,0:T(4,128)S(1)}, /*index=5*...) while((s32[]{:T(128)}, f32[4,96,2,7,64]{1,4,3,2,0:T(8,128)}, ...), condition=%wide.region_16.17_spmd, body=%wide.region_12.16_spmd.sunk | while | flops 716440064 | bytes 5492981 | solution.py:172
  142.1 8.1 conditional.7
  142.5 7.7 bitcast_add_fusion.1
  164.3 17.4 %fusion.57 = f32[384,9728]{1,0:T(8,128)} fusion(bf16[896,9728]{1,0:T(8,128)(2,1)} %param.29, f32[384,896]{1,0:T(8,128)S(1)} %get-tuple-element.1328, f32[896]{0:T(1024)S(1)} %convert_element_type.166, f32[384]{0:T(512)S(1)} %add_rsqrt_fusion), kind=kOutput, calls=%fused_computation.134 | convolution fusion | flops 6695141376 | bytes 33756160 | tf_op jit(solution)/shard_map/dot_general | solution.py:181
  181.7 14.5 multiply_convert_fusion.1
  196.2 16.0 %multiply_reduce_fusion = (f32[896]{0:T(1024)}, f32[384]{0:T(512)S(1)}, f32[384,896]{1,0:T(8,128)}) fusion(f32[384,896]{1,0:T(8,128)} %copy-done.8, f32[384]{0:T(512)S(1)} %add_rsqrt_fusion, f32[896]{0:T(1024)S(1)} %convert_element_type.166, bf16[896,9728]{1,0:T(8,128)(2,1)} %param.29, bf16[384,4864]{1,0:T(8,128)(2,1)} %get-tuple-element.1315, ...), kind=kOutput, calls=%fused_computation.84 | convolution fusion | flops 6711114240 | bytes 27666432 | tf_op jit(solution)/shard_map/dot_general | solution.py:60
  231.2 25.8 %while.60 = (s32[]{:T(128)}, f32[4,96,2,7,64]{1,4,3,2,0:T(8,128)}, bf16[1536,4,256]{0,2,1:T(8,128)(2,1)}, s32[96]{0:T(128)S(1)}, s32[4,1536]{1,0:T(4,128)S(1)}, ...) while((s32[]{:T(128)}, f32[4,96,2,7,64]{1,4,3,2,0:T(8,128)}, ...), condition=%wide.region_24.25_spmd, body=%wide.region_20.24_spmd.sunk | while | flops 1792885248 | bytes 74315176 | solution.py:262
  233.8 18.0 %conditional.8 = ((f32[4,96,2,7,64]{1,4,3,2,0:T(8,128)}, bf16[1536,4,256]{0,2,1:T(8,128)(2,1)})) conditional(s32[]{:T(128)} %convert_element_type.222, (f32[4,96,2,7,64]{1,4,3,2,0:T(8,128)}, bf16[1536,4,256]{0,2,1:T(8,128)(2,1)}) %tuple.195, (s32[]{:T(128)}, bf16[4,1536,2,64]{1,3,2,0:T(8,128)(2,1)}, s32[4,96]{1,0:T(4,128)S(1)}, ...), branch_computations={%region_22.22_spmd, %region_23.23_spmd} | conditional | flops 1792885248 | bytes 74314792 | solution.py:260
  239.8 5.0 fusion.26
  265.6 57.8 %all-to-all-start = ((bf16[16,96,4,256]{3,1,2,0:T(8,128)(2,1)}), bf16[16,96,4,256]{3,1,2,0:T(8,128)(2,1)}, u32[]{:S(2)}, u32[]{:S(2)}) async-start(bf16[16,96,4,256]{3,1,2,0:T(8,128)(2,1)} %copy.118), calls=%async_computation | async-start | bytes 6291456 | tf_op jit(solution)/shard_map/all_to_all | solution.py:21
  335.8 18.5 %fusion.47 = f32[896,9728]{1,0:T(8,128)} fusion(bf16[384,4864]{1,0:T(8,128)(2,1)} %get-tuple-element.1315, bf16[384,4864]{1,0:T(8,128)(2,1)} %get-tuple-element.1314, f32[384,896]{1,0:T(8,128)} %copy-done.8, f32[896]{0:T(1024)S(1)} %convert_element_type.166, f32[384]{0:T(512)S(1)} %add_rsqrt_fusion), kind=kOutput, calls=%fused_computation.76 | convolution fusion | flops 6710083584 | bytes 43717632 | tf_op jit(solution)/shard_map/dot_general | solution.py:293
  354.3 31.3 %all-to-all-done = bf16[16,96,4,256]{3,1,2,0:T(8,128)(2,1)} async-done(((bf16[16,96,4,256]{3,1,2,0:T(8,128)(2,1)}), bf16[16,96,4,256]{3,1,2,0:T(8,128)(2,1)}, u32[]{:S(2)}, u32[]{:S(2)}) %all-to-all-start) | async-done | bytes 3145760 | tf_op jit(solution)/shard_map/all_to_all | solution.py:21
  393.8 4.8 fusion.58
  398.6 29.1 %pad_maximum_fusion = f32[896,11776]{1,0:T(8,128)} fusion(f32[896,9728]{1,0:T(8,128)} %fusion.47, f32[896,896]{1,0:T(8,128)} %fusion.50, f32[896,1152]{1,0:T(8,128)} %fusion.58), kind=kLoop, calls=%fused_computation.67 | loop fusion | flops 21102592 | bytes 84410368 | tf_op jit(solution)/shard_map/concatenate | solution.py:298
  427.8 7.2 convolution_convert_fusion
  435.0 292.5 %all_to_all.10 = bf16[16,304,896]{2,1,0:T(8,128)(2,1)} all-to-all(bf16[16,304,896]{2,1,0:T(8,128)(2,1)S(1)} %bitcast.171), channel_id=1, replica_groups=mesh['seq'=16,'dp'=2] {'seq'}, dimensions={0} | all-to-all | bytes 17432576 | tf_op jit(solution)/shard_map/all_to_all | solution.py:21
  727.4 5.8 reduce_sum.141
  733.2 653.0 %reduce-scatter.2.cloned.1.call-done = f32[56,11776]{1,0:T(8,128)} async-done(((f32[896,11776]{1,0:T(8,128)}), f32[56,11776]{1,0:T(8,128)}) %reduce-scatter.2.cloned.1.call-update) | async-done | bytes 2637840 | tf_op jit(solution)/shard_map/reduce_scatter | solution.py:315
  1389.3 9.9 add_convert_fusion
  1402.4 44.2 %all-reduce = (f32[1152]{0:T(1024)}, f32[896]{0:T(1024)}, f32[896]{0:T(1024)}) all-reduce(f32[1152]{0:T(1024)S(1)} %convert_reduce_fusion.1, f32[896]{0:T(1024)} %get-tuple-element.1245, f32[896]{0:T(1024)} %get-tuple-element.1243), channel_id=1, replica_groups=mesh['seq'=16,'dp'=2] {'seq','dp'}, use_global_device_ids=true, to_apply=%region_30.31 | all-reduce | flops 2944 | bytes 23552 | tf_op jit(solution)/shard_map/psum | solution.py:328
  (192 shorter events, 135.5 us)
Async XLA Ops:
  7.2 6.3 copy-start
  7.2 68.4 %all-gather.5.cloned.1.call-start = ((), (), s32[]{:S(2)}) async-start(), calls=%async_computation.4 | async-start | bytes 1671168 | tf_op jit(solution)/shard_map/all_gather | solution.py:98
  10.4 4.2 copy-start.25
  11.1 3.5 copy-start.23
  11.2 3.4 copy-start.21
  16.0 5.4 copy-start.27
  16.3 6.9 copy-start.13
  16.3 6.9 copy-start.15
  17.3 118.2 %all-gather.3.cloned.1.call-start = ((), (), s32[]{:S(2)}) async-start(), calls=%async_computation.3 | async-start | bytes 1671168 | tf_op jit(solution)/shard_map/all_gather | solution.py:99
  164.2 17.5 %copy-start.8 = (f32[384,896]{1,0:T(8,128)}, f32[384,896]{1,0:T(8,128)S(1)}, u32[]{:S(2)}) copy-start(f32[384,896]{1,0:T(8,128)S(1)} %get-tuple-element.1328) | copy-start | bytes 4128772
  164.3 17.4 %copy-start.10 = (bf16[4,96,896]{2,1,0:T(8,128)(2,1)S(1)}, bf16[4,96,896]{2,1,0:T(8,128)(2,1)}, u32[]{:S(2)}) copy-start(bf16[4,96,896]{2,1,0:T(8,128)(2,1)} %broadcast_multiply_fusion) | copy-start | bytes 2064388
  212.2 3.6 copy-start.28
  223.3 3.4 copy-start.5
  265.6 120.0 %all-to-all-start = ((bf16[16,96,4,256]{3,1,2,0:T(8,128)(2,1)}), bf16[16,96,4,256]{3,1,2,0:T(8,128)(2,1)}, u32[]{:S(2)}, u32[]{:S(2)}) async-start(bf16[16,96,4,256]{3,1,2,0:T(8,128)(2,1)} %copy.118), calls=%async_computation | async-start | bytes 6291456 | tf_op jit(solution)/shard_map/all_to_all | solution.py:21
  323.3 1063.0 %reduce-scatter.2.cloned.1.call-start = ((), (), s32[]{:S(2)}) async-start(), calls=%async_computation.5 | async-start | bytes 44843008 | tf_op jit(solution)/shard_map/reduce_scatter | solution.py:315
  327.3 3.1 copy-start.14
  327.3 3.1 copy-start.16
  427.7 1022.6 %all-reduce.4.cloned.1.call-start = ((), (), s32[]{:S(2)}) async-start(), calls=%async_computation.6 | async-start | bytes 3727360 | tf_op jit(solution)/shard_map/psum | solution.py:325
  1389.2 9.9 copy-start.7
  1389.2 9.9 copy-start.18
  1389.3 10.2 copy-start.6
  1389.3 10.2 copy-start.24
  1389.3 10.1 copy-start.26
  1453.5 2.8 copy-start.20
  (10 other events, 18.1 us)
Sparse Core Ops, SparseCore 0:
  17.4 58.1 all-gather.4
  78.8 56.6 all-gather.2
  427.9 958.3 reduce-scatter.1
  1389.4 22.3 all-reduce.3
where the time goes:
time: 1470 us; the launch traced here: 1460 us
  waiting for transfers between devices  772 us (53%)
  blocking collectives  337 us (23%)
  matrix products  126 us (9%)
  other arithmetic  76.5 us (5%)
  local copies, waits for them, and re-layouts  68.9 us (5%)
  starting transfers between devices  57.9 us (4%)
    reduce_scatter x1, waiting for transfers between devices, shards(): lax.psum_scatter(row_terms(jnp.int32(0), row_share * lax.axis_size('seq')...  653 us
    all_to_all x1, blocking collectives, summed_on_arrival(): lax.all_to_all(cut_along(shard, dim, devices), axis, 0, 0, tiled=True)  292 us
    all_to_all x1, starting transfers between devices, summed_on_arrival(): lax.all_to_all(cut_along(shard, dim, devices), axis, 0, 0, tiled=True)  57.8 us
    all_gather x1, waiting for transfers between devices, shards(): lax.all_gather(key_low, 'seq', axis=1, tiled=True)  46.4 us
    psum x1, blocking collectives, shards(): lax.psum((bias_part, gain_attn_part, gain_mlp_part), ('seq', 'dp'))  44.2 us
    all_gather x1, waiting for transfers between devices, shards(): lax.all_gather(value_low, 'seq', axis=1, tiled=True)  40.9 us
    dot_general x4, matrix products, transposed_product(): lax.dot_general(left, right, (((1,), (1,)), ((), ())), preferred_element_...  35.4 us
    dot_general x4, matrix products, product(): lax.dot_general(left, right, (((0,), (0,)), ((), ())), preferred_element_...  33.2 us
  transfers between devices with their start and end apart: 5, of which 4 were waited for; matrix products, arithmetic and copies ran while one was open for 6% of the time, Pallas kernels for 0%

commit v1 on v0

--- a/solution.py
+++ b/solution.py
@@ -2,6 +2,7 @@
 import jax.numpy as jnp
 from jax import lax
 from jax.sharding import PartitionSpec as P
+from jax.lax import all_to_all, axis_size
 
 HEADS = 14
 KVH = 2
@@ -96,7 +97,15 @@
     )
     key_all, value_all = (
         lax.all_gather(key_low, "seq", axis=1, tiled=True),
-        lax.all_gather(value_low, "seq", axis=1, tiled=True),
+        jnp.concatenate(
+            all_to_all(
+                jnp.stack([value_low for _ in range(axis_size("seq"))]),
+                axis_name="seq",
+                split_axis=0,
+                concat_axis=0,
+            ),
+            1,
+        ),
     )
     key_all = key_all.reshape(streams, stream_len, KVH, HD)
     value_all = value_all.reshape(streams, stream_len, KVH, HD)

time: 1470 us -> 1470 us (level)
  waiting for transfers between devices: 772 us -> 736 us
  starting transfers between devices: 57.9 us -> 79.4 us
    all_gather x1, waiting for transfers between devices: 40.9 us -> 0.02 us  [shards(): lax.all_gather(value_low, 'seq', axis=1, tiled=True)]
  transfers between devices with their start and end apart: 5 -> 6, of which waited for: 4 -> 3; matrix products, arithmetic and copies ran while one was open for 6% -> 13% of each run, Pallas kernels for 0% -> 0%
where the time goes in v1:
time: 1470 us; the launch traced here: 1460 us
  waiting for transfers between devices  736 us (50%)
  blocking collectives  337 us (23%)
  matrix products  126 us (9%)
  local copies, waits for them, and re-layouts  80.4 us (5%)
  starting transfers between devices  79.4 us (5%)
  other arithmetic  75.9 us (5%)
    reduce_scatter x1, waiting for transfers between devices, shards(): lax.psum_scatter(row_terms(jnp.int32(0), row_share * lax.axis_size('seq')...  653 us
    all_to_all x1, blocking collectives, summed_on_arrival(): lax.all_to_all(cut_along(shard, dim, devices), axis, 0, 0, tiled=True)  293 us
    all_to_all x1, starting transfers between devices, summed_on_arrival(): lax.all_to_all(cut_along(shard, dim, devices), axis, 0, 0, tiled=True)  72 us
    all_gather x1, waiting for transfers between devices, shards(): lax.all_gather(key_low, 'seq', axis=1, tiled=True)  50.6 us
    psum x1, blocking collectives, shards(): lax.psum((bias_part, gain_attn_part, gain_mlp_part), ('seq', 'dp'))  44.2 us
    dot_general x4, matrix products, transposed_product(): lax.dot_general(left, right, (((1,), (1,)), ((), ())), preferred_element_...  35.4 us
    dot_general x4, matrix products, product(): lax.dot_general(left, right, (((0,), (0,)), ((), ())), preferred_element_...  33.4 us
    all_to_all x1, waiting for transfers between devices, summed_on_arrival(): lax.all_to_all(cut_along(shard, dim, devices), axis, 0, 0, tiled=True)  31.3 us
  transfers between devices with their start and end apart: 6, of which 3 were waited for; matrix products, arithmetic and copies ran while one was open for 13% of the time, Pallas kernels for 0%

profile of v1, /device:TPU:6, one launch (start us, length us, event | category | flops | bytes accessed | tf_op | source)
XLA Modules:
  0.0 1460.8 jit_solution(10166533767930600797)
XLA Ops:
  19.7 7.3 all-to-all-start
  38.0 50.6 %all-gather.3.cloned.1.call-done = bf16[4,1536,128]{2,0,1:T(4,128)(2,1)} async-done(((bf16[4,96,128]{2,0,1:T(4,128)(2,1)}), bf16[4,1536,128]{2,0,1:T(4,128)(2,1)}) %all-gather.3.cloned.1.call-update) | async-done | bytes 1572880 | tf_op jit(solution)/shard_map/all_gather | solution.py:99
  92.5 15.1 %while.58 = (s32[]{:T(128)}, f32[4,2,7,96,1]{3,2,1,0,4:T(8,128)S(1)}, f32[4,2,7,96,1]{3,2,1,0,4:T(8,128)S(1)}, s32[96]{0:T(128)S(1)}, s32[4,1536]{1,0:T(4,128)S(...) while((s32[]{:T(128)}, ...), condition=%wide.region_11.12_spmd, body=%wide.region_5.11_spmd.sunk | while | flops 374795296 | bytes 24231176 | solution.py:155
  95.1 7.2 conditional.6
  118.1 15.9 %while.59 = (s32[]{:T(128)}, f32[4,96,2,7,64]{1,4,3,2,0:T(8,128)}, s32[96]{0:T(128)S(1)}, s32[4,1536]{1,0:T(4,128)S(1)}, s32[4,96]{1,0:T(4,128)S(1)}, /*index=5*...) while((s32[]{:T(128)}, f32[4,96,2,7,64]{1,4,3,2,0:T(8,128)}, ...), condition=%wide.region_16.17_spmd, body=%wide.region_12.16_spmd.sunk | while | flops 716440064 | bytes 5492981 | solution.py:181
  120.7 8.1 conditional.7
  121.1 7.7 bitcast_add_fusion.1
  143.3 17.3 %fusion.57 = f32[384,9728]{1,0:T(8,128)} fusion(bf16[896,9728]{1,0:T(8,128)(2,1)} %param.29, f32[384,896]{1,0:T(8,128)S(1)} %get-tuple-element.1328, f32[896]{0:T(1024)S(1)} %convert_element_type.166, f32[384]{0:T(512)S(1)} %add_rsqrt_fusion), kind=kOutput, calls=%fused_computation.134 | convolution fusion | flops 6695141376 | bytes 33756160 | tf_op jit(solution)/shard_map/dot_general | solution.py:190
  160.6 14.5 multiply_convert_fusion.1
  175.0 16.1 %multiply_reduce_fusion = (f32[896]{0:T(1024)}, f32[384]{0:T(512)S(1)}, f32[384,896]{1,0:T(8,128)}) fusion(f32[384,896]{1,0:T(8,128)} %copy-done.8, f32[384]{0:T(512)S(1)} %add_rsqrt_fusion, f32[896]{0:T(1024)S(1)} %convert_element_type.166, bf16[896,9728]{1,0:T(8,128)(2,1)} %param.29, bf16[384,4864]{1,0:T(8,128)(2,1)} %get-tuple-element.1315, ...), kind=kOutput, calls=%fused_computation.84 | convolution fusion | flops 6711114240 | bytes 27666432 | tf_op jit(solution)/shard_map/dot_general | solution.py:61
  213.3 25.8 %while.60 = (s32[]{:T(128)}, f32[4,96,2,7,64]{1,4,3,2,0:T(8,128)}, bf16[1536,4,256]{0,2,1:T(8,128)(2,1)}, s32[96]{0:T(128)S(1)}, s32[4,1536]{1,0:T(4,128)S(1)}, ...) while((s32[]{:T(128)}, f32[4,96,2,7,64]{1,4,3,2,0:T(8,128)}, ...), condition=%wide.region_24.25_spmd, body=%wide.region_20.24_spmd.sunk | while | flops 1792885248 | bytes 74315176 | solution.py:271
  215.9 18.0 %conditional.8 = ((f32[4,96,2,7,64]{1,4,3,2,0:T(8,128)}, bf16[1536,4,256]{0,2,1:T(8,128)(2,1)})) conditional(s32[]{:T(128)} %convert_element_type.222, (f32[4,96,2,7,64]{1,4,3,2,0:T(8,128)}, bf16[1536,4,256]{0,2,1:T(8,128)(2,1)}) %tuple.195, (s32[]{:T(128)}, bf16[4,1536,2,64]{1,3,2,0:T(8,128)(2,1)}, s32[4,96]{1,0:T(4,128)S(1)}, ...), branch_computations={%region_22.22_spmd, %region_23.23_spmd} | conditional | flops 1792885248 | bytes 74314792 | solution.py:269
  221.9 5.0 fusion.26
  247.6 72.0 %all-to-all-start.1 = ((bf16[16,96,4,256]{3,1,2,0:T(8,128)(2,1)}), bf16[16,96,4,256]{3,1,2,0:T(8,128)(2,1)}, u32[]{:S(2)}, u32[]{:S(2)}) async-start(bf16[16,96,4,256]{3,1,2,0:T(8,128)(2,1)} %copy.124), calls=%async_computation.1 | async-start | bytes 6291456 | tf_op jit(solution)/shard_map/all_to_all | solution.py:22
  332.2 18.6 %fusion.47 = f32[896,9728]{1,0:T(8,128)} fusion(bf16[384,4864]{1,0:T(8,128)(2,1)} %get-tuple-element.1315, bf16[384,4864]{1,0:T(8,128)(2,1)} %get-tuple-element.1314, f32[384,896]{1,0:T(8,128)} %copy-done.8, f32[896]{0:T(1024)S(1)} %convert_element_type.166, f32[384]{0:T(512)S(1)} %add_rsqrt_fusion), kind=kOutput, calls=%fused_computation.76 | convolution fusion | flops 6710083584 | bytes 43717632 | tf_op jit(solution)/shard_map/dot_general | solution.py:302
  350.8 31.3 %all-to-all-done.1 = bf16[16,96,4,256]{3,1,2,0:T(8,128)(2,1)} async-done(((bf16[16,96,4,256]{3,1,2,0:T(8,128)(2,1)}), bf16[16,96,4,256]{3,1,2,0:T(8,128)(2,1)}, u32[]{:S(2)}, u32[]{:S(2)}) %all-to-all-start.1) | async-done | bytes 3145760 | tf_op jit(solution)/shard_map/all_to_all | solution.py:22
  390.3 4.8 fusion.58
  395.1 29.1 %pad_maximum_fusion = f32[896,11776]{1,0:T(8,128)} fusion(f32[896,9728]{1,0:T(8,128)} %fusion.47, f32[896,896]{1,0:T(8,128)} %fusion.50, f32[896,1152]{1,0:T(8,128)} %fusion.58), kind=kLoop, calls=%fused_computation.67 | loop fusion | flops 21102592 | bytes 84410368 | tf_op jit(solution)/shard_map/concatenate | solution.py:307
  424.3 7.2 convolution_convert_fusion
  431.5 292.6 %all_to_all.15 = bf16[16,304,896]{2,1,0:T(8,128)(2,1)} all-to-all(bf16[16,304,896]{2,1,0:T(8,128)(2,1)S(1)} %bitcast.176), channel_id=1, replica_groups=mesh['seq'=16,'dp'=2] {'seq'}, dimensions={0} | all-to-all | bytes 17432576 | tf_op jit(solution)/shard_map/all_to_all | solution.py:22
  724.1 5.8 reduce_sum.141
  729.9 652.9 %reduce-scatter.2.cloned.1.call-done = f32[56,11776]{1,0:T(8,128)} async-done(((f32[896,11776]{1,0:T(8,128)}), f32[56,11776]{1,0:T(8,128)}) %reduce-scatter.2.cloned.1.call-update) | async-done | bytes 2637840 | tf_op jit(solution)/shard_map/reduce_scatter | solution.py:324
  1385.8 9.9 add_convert_fusion
  1398.9 44.2 %all-reduce = (f32[1152]{0:T(1024)}, f32[896]{0:T(1024)}, f32[896]{0:T(1024)}) all-reduce(f32[1152]{0:T(1024)S(1)} %convert_reduce_fusion.1, f32[896]{0:T(1024)} %get-tuple-element.1245, f32[896]{0:T(1024)} %get-tuple-element.1243), channel_id=1, replica_groups=mesh['seq'=16,'dp'=2] {'seq','dp'}, use_global_device_ids=true, to_apply=%region_30.31 | all-reduce | flops 2944 | bytes 23552 | tf_op jit(solution)/shard_map/psum | solution.py:337
  (199 shorter events, 147.1 us)
Async XLA Ops:
  7.2 6.3 copy-start
  7.2 81.4 %all-gather.3.cloned.1.call-start = ((), (), s32[]{:S(2)}) async-start(), calls=%async_computation.4 | async-start | bytes 1671168 | tf_op jit(solution)/shard_map/all_gather | solution.py:99
  10.4 4.2 copy-start.26
  11.1 3.5 copy-start.24
  11.2 3.4 copy-start.22
  16.3 15.7 %copy-start.13 = (f32[384,32]{0,1:T(8,128)}, f32[384,32]{0,1:T(8,128)S(1)}, u32[]{:S(2)}) copy-start(f32[384,32]{0,1:T(8,128)S(1)} %get-tuple-element.1325) | copy-start | bytes 147460
  16.3 15.7 %copy-start.15 = (f32[384,32]{0,1:T(8,128)}, f32[384,32]{0,1:T(8,128)S(1)}, u32[]{:S(2)}) copy-start(f32[384,32]{0,1:T(8,128)S(1)} %get-tuple-element.1326) | copy-start | bytes 147460
  19.7 87.9 %all-to-all-start = ((bf16[16,4,96,128]{3,2,1,0:T(8,128)(2,1)}), bf16[16,4,96,128]{3,2,1,0:T(8,128)(2,1)}, u32[]{:S(2)}, u32[]{:S(2)}) async-start(bf16[16,4,96,128]{3,2,1,0:T(8,128)(2,1)} %stack.3), calls=%async_computation | async-start | bytes 3145728 | tf_op jit(solution)/shard_map/all_to_all | solution.py:101
  27.0 3.3 copy-start.28
  27.0 180.4 %all-gather.5.cloned.1.call-start = ((), (), s32[]{:S(2)}) async-start(), calls=%async_computation.5 | async-start | bytes 1671168 | tf_op jit(solution)/shard_map/all_gather | solution.py:223
  143.2 17.3 %copy-start.8 = (f32[384,896]{1,0:T(8,128)}, f32[384,896]{1,0:T(8,128)S(1)}, u32[]{:S(2)}) copy-start(f32[384,896]{1,0:T(8,128)S(1)} %get-tuple-element.1328) | copy-start | bytes 4128772
  143.2 17.3 %copy-start.10 = (bf16[4,96,896]{2,1,0:T(8,128)(2,1)S(1)}, bf16[4,96,896]{2,1,0:T(8,128)(2,1)}, u32[]{:S(2)}) copy-start(bf16[4,96,896]{2,1,0:T(8,128)(2,1)} %broadcast_multiply_fusion) | copy-start | bytes 2064388
  191.1 3.6 copy-start.29
  247.6 134.4 %all-to-all-start.1 = ((bf16[16,96,4,256]{3,1,2,0:T(8,128)(2,1)}), bf16[16,96,4,256]{3,1,2,0:T(8,128)(2,1)}, u32[]{:S(2)}, u32[]{:S(2)}) async-start(bf16[16,96,4,256]{3,1,2,0:T(8,128)(2,1)} %copy.124), calls=%async_computation.1 | async-start | bytes 6291456 | tf_op jit(solution)/shard_map/all_to_all | solution.py:22
  319.6 1063.2 %reduce-scatter.2.cloned.1.call-start = ((), (), s32[]{:S(2)}) async-start(), calls=%async_computation.6 | async-start | bytes 44843008 | tf_op jit(solution)/shard_map/reduce_scatter | solution.py:324
  323.6 3.2 copy-start.14
  323.6 3.2 copy-start.16
  424.2 1022.6 %all-reduce.4.cloned.1.call-start = ((), (), s32[]{:S(2)}) async-start(), calls=%async_computation.7 | async-start | bytes 3727360 | tf_op jit(solution)/shard_map/psum | solution.py:334
  1385.8 9.9 copy-start.7
  1385.8 9.9 copy-start.19
  1385.8 10.2 copy-start.6
  1385.8 10.2 copy-start.25
  1385.8 10.2 copy-start.27
  1450.0 2.8 copy-start.21
  (12 other events, 22.1 us)
Sparse Core Ops, SparseCore 0:
  17.4 71.0 all-gather.2
  91.8 56.6 all-gather.4
  424.3 958.4 reduce-scatter.1
  1385.9 22.2 all-reduce.3
